TPU v7x, 32 devices: a whole 2x2x4 slice. The times are simulated.
32 devices in a mesh: ctx: 16 (over z, x, core), chan: 2 (over y).
Axes of the slice: x: 2, y: 2, z: 4, core: 2. Of those that a mesh axis runs over, the one named last changes fastest.
Arguments:
- query_act: bfloat16 [2048, 1024], P('ctx', 'chan'), may hold values from -6 to 6
- key_act: bfloat16 [2048, 1024], P('ctx', 'chan'), may hold values from -6 to 6
- value_act: bfloat16 [2048, 1024], P('ctx', 'chan'), may hold values from -6 to 6
- filters: bfloat16 [2048, 1024], P('ctx', 'chan'), may hold values from -0.125 to 0.125
- skip_scale: float32 [1024], P('chan'), may hold values from -4 to 4
- w_out: bfloat16 [1024, 4096], P('chan'), may hold values from -0.25 to 0.25
Outputs:
- projected: bfloat16 [2048, 4096], P('ctx', 'chan')
All inputs are finite; a program needn't handle non-finite values.
Results may differ from a plain program's by a relative error of at most 0.015.
Values may be sent and summed in bfloat16 or wider, within the bound.
A program may use at most 64 MiB of HBM per device.

v0:
```python
import math
import jax
import jax.numpy as jnp
from jax import lax
from jax.sharding import PartitionSpec as P

precise = lax.Precision.HIGHEST


def phase_table(row_count, col_count, modulus, factor):
    row_index = lax.broadcasted_iota(jnp.int32, (row_count, col_count), 0)
    col_index = lax.broadcasted_iota(jnp.int32, (row_count, col_count), 1)
    phase_angle = (row_index * col_index % modulus).astype(jnp.float32) * (2.0 * math.pi / modulus)
    return (jnp.cos(phase_angle) * factor, jnp.sin(phase_angle) * factor)


def twiddle(freq_index, pos_index, modulus):
    phase_angle = (freq_index * pos_index % modulus).astype(jnp.float32) * (2.0 * math.pi / modulus)
    return (jnp.cos(phase_angle), jnp.sin(phase_angle))


def shards(query_act, key_act, value_act, filters, skip_scale, w_out):
    tok_rows, chan_width = key_act.shape
    ctx_size = lax.axis_size("ctx")
    per_dev = tok_rows // ctx_size
    fft_length = 2 * tok_rows * ctx_size
    freq_blocks = 2 * ctx_size
    ctx_index = lax.axis_index("ctx")
    gated_in = (key_act.astype(jnp.float32) * value_act.astype(jnp.float32)).astype(jnp.bfloat16)
    sent_input, sent_filter = (
        lax.all_to_all(
            gated_in.reshape(1, ctx_size, per_dev, chan_width),
            "ctx",
            split_axis=1,
            concat_axis=0,
            tiled=True,
        ),
        lax.all_to_all(
            filters.reshape(1, ctx_size, per_dev, chan_width),
            "ctx",
            split_axis=1,
            concat_axis=0,
            tiled=True,
        ),
    )
    block_cos, block_sin = phase_table(freq_blocks, ctx_size, freq_blocks, 1.0)
    offsets = ctx_index * per_dev + lax.broadcasted_iota(jnp.int32, (1, per_dev), 1)
    all_freq = lax.broadcasted_iota(jnp.int32, (freq_blocks, 1), 0)
    front_cos, front_sin = twiddle(all_freq, offsets, fft_length)
    front_cos = front_cos[:, :, None]
    front_sin = front_sin[:, :, None]

    def first_section(signal):
        values32 = signal.reshape(ctx_size, per_dev, chan_width).astype(jnp.float32)
        real_part = jnp.einsum("kp,pjc->kjc", block_cos, values32, precision=precise)
        imag_part = -jnp.einsum("kp,pjc->kjc", block_sin, values32, precision=precise)
        out_real = real_part * front_cos + imag_part * front_sin
        out_imag = imag_part * front_cos - real_part * front_sin
        return jnp.stack([out_real, out_imag]).reshape(2, ctx_size, 2, per_dev, chan_width)

    cycle_cos, cycle_sin = phase_table(tok_rows, tok_rows, tok_rows, 1.0)

    def cycle_apply(table, operand):
        return jnp.einsum("kn,zmnc->zmkc", table, operand, precision=precise)

    spec_input = lax.all_to_all(
        first_section(sent_input), "ctx", split_axis=1, concat_axis=3, tiled=True
    )
    spec_filter = lax.all_to_all(
        first_section(sent_filter), "ctx", split_axis=1, concat_axis=3, tiled=True
    )

    def forward(portion):
        real_in = portion[0]
        imag_in = portion[1]
        out_real = cycle_apply(cycle_cos, real_in) + cycle_apply(cycle_sin, imag_in)
        out_imag = cycle_apply(cycle_cos, imag_in) - cycle_apply(cycle_sin, real_in)
        return (out_real, out_imag)

    input_real, input_imag = forward(spec_input)
    filter_real, filter_imag = forward(spec_filter)
    prod_real = input_real * filter_real - input_imag * filter_imag
    prod_imag = input_real * filter_imag + input_imag * filter_real
    back_real = cycle_apply(cycle_cos, prod_real) - cycle_apply(cycle_sin, prod_imag)
    back_imag = cycle_apply(cycle_cos, prod_imag) + cycle_apply(cycle_sin, prod_real)
    mixed = jnp.stack([back_real, back_imag])
    inverted = mixed[:, 0]
    pack_width = inverted.shape[-1]
    own_freq = 2 * ctx_index + lax.broadcasted_iota(jnp.int32, (2, 1), 0)
    all_offsets = lax.broadcasted_iota(jnp.int32, (1, tok_rows), 1)
    back_cos, back_sin = twiddle(own_freq, all_offsets, fft_length)
    back_cos = back_cos[:, :, None]
    back_sin = back_sin[:, :, None]
    turned_real = inverted[0] * back_cos - inverted[1] * back_sin
    turned_imag = inverted[0] * back_sin + inverted[1] * back_cos
    turned = jnp.stack([turned_real, turned_imag]).reshape(2, 2, ctx_size, per_dev, pack_width)
    last_cos, last_sin = phase_table(ctx_size, freq_blocks, freq_blocks, 1.0 / fft_length)

    def last_apply(table, operand):
        return jnp.einsum("nk,kzmc->nzmc", table, operand, precision=precise)

    portion = lax.all_to_all(turned, "ctx", split_axis=2, concat_axis=1, tiled=True)
    returned = last_apply(last_cos, portion[0]) - last_apply(last_sin, portion[1])
    convolved = lax.all_to_all(returned, "ctx", split_axis=0, concat_axis=1, tiled=True).reshape(
        tok_rows, chan_width
    )
    gated = (
        query_act.astype(jnp.float32)
        * (convolved + skip_scale[None, :] * gated_in.astype(jnp.float32))
    ).astype(jnp.bfloat16)
    summed = lax.psum_scatter(
        lax.dot_general(
            w_out, gated, (((0,), (1,)), ((), ())), preferred_element_type=jnp.float32
        ).astype(jnp.bfloat16),
        "chan",
        scatter_dimension=0,
        tiled=True,
    )
    return summed.T


def solution(mesh):
    return jax.shard_map(
        shards,
        mesh=mesh,
        in_specs=(
            P("ctx", "chan"),
            P("ctx", "chan"),
            P("ctx", "chan"),
            P("ctx", "chan"),
            P("chan"),
            P("chan", None),
        ),
        out_specs=P("ctx", "chan"),
        check_vma=False,
    )
```

profile of v0, /device:TPU:0, one launch (start us, length us, event | category | flops | bytes accessed | tf_op | source)
XLA Modules:
  0.0 180.7 jit_solution(6431051070737040364)
XLA Ops:
  6.5 1.7 fusion.49
  8.2 7.4 %all-to-all-start = ((bf16[1,16,8,512]{3,2,0,1:T(8,128)(2,1)}), bf16[1,16,8,512]{3,2,0,1:T(8,128)(2,1)S(1)}, u32[]{:S(2)}, u32[]{:S(2)}) async-start(bf16[1,16,8,512]{3,2,0,1:T(8,128)(2,1)} %fusion.49), calls=%async_computation | async-start | bytes 262144 | tf_op jit(solution)/shard_map/all_to_all | solution.py:31
  15.7 7.8 %all-to-all-done = bf16[1,16,8,512]{3,2,0,1:T(8,128)(2,1)S(1)} async-done(((bf16[1,16,8,512]{3,2,0,1:T(8,128)(2,1)}), bf16[1,16,8,512]{3,2,0,1:T(8,128)(2,1)S(1)}, u32[]{:S(2)}, u32[]{:S(2)}) %all-to-all-start) | async-done | bytes 131104 | tf_op jit(solution)/shard_map/all_to_all | solution.py:31
  23.5 3.5 %all-to-all-start.2 = ((bf16[1,16,8,512]{3,2,0,1:T(8,128)(2,1)}), bf16[1,16,8,512]{3,2,0,1:T(8,128)(2,1)S(1)}, u32[]{:S(2)}, u32[]{:S(2)}) async-start(bf16[1,16,8,512]{3,2,0,1:T(8,128)(2,1)} %bitcast.166), calls=%async_computation.2 | async-start | bytes 262144 | tf_op jit(solution)/shard_map/all_to_all | solution.py:38
  27.0 0.5 convolution_negate_fusion.1
  27.5 0.5 fusion.24
  28.0 6.9 %all-to-all-done.2 = bf16[1,16,8,512]{3,2,0,1:T(8,128)(2,1)S(1)} async-done(((bf16[1,16,8,512]{3,2,0,1:T(8,128)(2,1)}), bf16[1,16,8,512]{3,2,0,1:T(8,128)(2,1)S(1)}, u32[]{:S(2)}, u32[]{:S(2)}) %all-to-all-start.2) | async-done | bytes 131104 | tf_op jit(solution)/shard_map/all_to_all | solution.py:38
  35.4 0.6 multiply_add_fusion.1
  36.7 1.1 pad_maximum_fusion.1
  37.8 3.7 %all-to-all-start.3 = ((f32[2,16,2,8,512]{4,3,2,0,1:T(8,128)}), f32[2,16,2,8,512]{4,3,2,0,1:T(8,128)S(1)}, u32[]{:S(2)}, u32[]{:S(2)}) async-start(f32[2,16,2,8,512]{4,3,2,0,1:T(8,128)} %pad_maximum_fusion.1), calls=%async_computation.3 | async-start | bytes 2097152 | tf_op jit(solution)/shard_map/all_to_all | solution.py:69
  42.1 1.1 pad_maximum_fusion
  43.1 21.2 %all-to-all-done.3 = f32[2,16,2,8,512]{4,3,2,0,1:T(8,128)S(1)} async-done(((f32[2,16,2,8,512]{4,3,2,0,1:T(8,128)}), f32[2,16,2,8,512]{4,3,2,0,1:T(8,128)S(1)}, u32[]{:S(2)}, u32[]{:S(2)}) %all-to-all-start.3) | async-done | bytes 1048608 | tf_op jit(solution)/shard_map/all_to_all | solution.py:69
  64.3 6.8 %all-to-all-start.1 = ((f32[2,16,2,8,512]{4,3,2,0,1:T(8,128)}), f32[2,16,2,8,512]{4,3,2,0,1:T(8,128)S(1)}, u32[]{:S(2)}, u32[]{:S(2)}) async-start(f32[2,16,2,8,512]{4,3,2,0,1:T(8,128)} %pad_maximum_fusion), calls=%async_computation.1 | async-start | bytes 2097152 | tf_op jit(solution)/shard_map/all_to_all | solution.py:66
  71.6 1.1 fusion.16
  72.7 1.1 fusion.15
  73.8 20.2 %all-to-all-done.1 = f32[2,16,2,8,512]{4,3,2,0,1:T(8,128)S(1)} async-done(((f32[2,16,2,8,512]{4,3,2,0,1:T(8,128)}), f32[2,16,2,8,512]{4,3,2,0,1:T(8,128)S(1)}, u32[]{:S(2)}, u32[]{:S(2)}) %all-to-all-start.1) | async-done | bytes 1048608 | tf_op jit(solution)/shard_map/all_to_all | solution.py:66
  94.2 1.1 fusion.14
  95.3 1.1 fusion.13
  96.4 1.1 convolution_subtract_fusion.1
  97.5 1.1 convolution_add_fusion.1
  98.7 1.1 convolution_add_fusion.2
  99.8 1.1 multiply_subtract_fusion
  100.9 0.9 fusion.8
  101.8 0.9 fusion.10
  102.7 0.9 fusion.1
  103.6 1.2 subtract_bitcast_fusion
  105.1 31.8 %all_to_all.72 = f32[2,2,16,8,512]{4,3,1,0,2:T(8,128)S(1)} all-to-all(f32[2,2,16,8,512]{4,3,1,0,2:T(8,128)S(1)} %copy.81), channel_id=1, replica_groups=mesh['ctx'=16,'chan'=2] {'ctx'}, dimensions={2} | all-to-all | bytes 2097152 | tf_op jit(solution)/shard_map/all_to_all | solution.py:102
  136.9 0.7 fusion.5
  137.6 0.7 fusion.3
  138.5 14.8 %all_to_all.73 = f32[16,1,8,512]{3,2,1,0:T(8,128)S(1)} all-to-all(f32[16,1,8,512]{3,2,1,0:T(8,128)S(1)} %copy.64), channel_id=1, replica_groups=mesh['ctx'=16,'chan'=2] {'ctx'}, dimensions={0} | all-to-all | bytes 524288 | tf_op jit(solution)/shard_map/all_to_all | solution.py:104
  153.3 1.7 fusion
  155.1 18.8 %reduce-scatter.2.cloned.1.call-done = bf16[2048,128]{0,1:T(8,128)(2,1)} async-done(((bf16[4096,128]{0,1:T(8,128)(2,1)}), bf16[2048,128]{0,1:T(8,128)(2,1)}) %reduce-scatter.2.cloned.1.call-update) | async-done | bytes 524304 | tf_op jit(solution)/shard_map/reduce_scatter | solution.py:111
  (27 shorter events, 2.8 us)
Async XLA Ops:
  8.2 15.3 %all-to-all-start = ((bf16[1,16,8,512]{3,2,0,1:T(8,128)(2,1)}), bf16[1,16,8,512]{3,2,0,1:T(8,128)(2,1)S(1)}, u32[]{:S(2)}, u32[]{:S(2)}) async-start(bf16[1,16,8,512]{3,2,0,1:T(8,128)(2,1)} %fusion.49), calls=%async_computation | async-start | bytes 262144 | tf_op jit(solution)/shard_map/all_to_all | solution.py:31
  23.5 11.4 %all-to-all-start.2 = ((bf16[1,16,8,512]{3,2,0,1:T(8,128)(2,1)}), bf16[1,16,8,512]{3,2,0,1:T(8,128)(2,1)S(1)}, u32[]{:S(2)}, u32[]{:S(2)}) async-start(bf16[1,16,8,512]{3,2,0,1:T(8,128)(2,1)} %bitcast.166), calls=%async_computation.2 | async-start | bytes 262144 | tf_op jit(solution)/shard_map/all_to_all | solution.py:38
  37.8 26.6 %all-to-all-start.3 = ((f32[2,16,2,8,512]{4,3,2,0,1:T(8,128)}), f32[2,16,2,8,512]{4,3,2,0,1:T(8,128)S(1)}, u32[]{:S(2)}, u32[]{:S(2)}) async-start(f32[2,16,2,8,512]{4,3,2,0,1:T(8,128)} %pad_maximum_fusion.1), calls=%async_computation.3 | async-start | bytes 2097152 | tf_op jit(solution)/shard_map/all_to_all | solution.py:69
  64.3 29.8 %all-to-all-start.1 = ((f32[2,16,2,8,512]{4,3,2,0,1:T(8,128)}), f32[2,16,2,8,512]{4,3,2,0,1:T(8,128)S(1)}, u32[]{:S(2)}, u32[]{:S(2)}) async-start(f32[2,16,2,8,512]{4,3,2,0,1:T(8,128)} %pad_maximum_fusion), calls=%async_computation.1 | async-start | bytes 2097152 | tf_op jit(solution)/shard_map/all_to_all | solution.py:66
  71.1 102.7 %reduce-scatter.2.cloned.1.call-start = ((), (), s32[]{:S(2)}) async-start(), calls=%async_computation.7 | async-start | bytes 1572864 | tf_op jit(solution)/shard_map/reduce_scatter | solution.py:111
  104.9 48.4 %copy-start = (bf16[512,4096]{1,0:T(8,128)(2,1)S(1)}, bf16[512,4096]{1,0:T(8,128)(2,1)}, u32[]{:S(2)}) copy-start(bf16[512,4096]{1,0:T(8,128)(2,1)} %param.11) | copy-start | bytes 12582916
  104.9 48.4 %copy-start.1 = (bf16[128,512]{1,0:T(8,128)(2,1)S(1)}, bf16[128,512]{1,0:T(8,128)(2,1)}, u32[]{:S(2)}) copy-start(bf16[128,512]{1,0:T(8,128)(2,1)} %param.8) | copy-start | bytes 393220
  104.9 48.4 %copy-start.2 = (bf16[128,512]{1,0:T(8,128)(2,1)S(1)}, bf16[128,512]{1,0:T(8,128)(2,1)}, u32[]{:S(2)}) copy-start(bf16[128,512]{1,0:T(8,128)(2,1)} %param.7) | copy-start | bytes 393220
  104.9 48.4 %copy-start.3 = (bf16[128,512]{1,0:T(8,128)(2,1)S(1)}, bf16[128,512]{1,0:T(8,128)(2,1)}, u32[]{:S(2)}) copy-start(bf16[128,512]{1,0:T(8,128)(2,1)} %param.6) | copy-start | bytes 393220
  105.0 48.4 %copy-start.4 = (f32[512]{0:T(512)S(1)}, f32[512]{0:T(512)}, u32[]{:S(2)}) copy-start(f32[512]{0:T(512)} %param.10) | copy-start | bytes 6148
Sparse Core Ops, SparseCore 0:
  155.2 18.6 reduce-scatter.1
where the time goes:
time: 181 us
  waiting for transfers between devices  75 us (41%)
  blocking collectives  46.6 us (26%)
  starting transfers between devices  21.6 us (12%)
  matrix products  17.9 us (10%)
  between operations  13.7 us (8%)
  other arithmetic  4.15 us (2%)
    all_to_all x1, blocking collectives, shards(): lax.all_to_all(turned, 'ctx', split_axis=2, concat_axis=1, tiled=True)  31.8 us
    all_to_all x1, waiting for transfers between devices, shards(): lax.all_to_all(first_section(sent_filter), 'ctx', split_axis=1, concat_ax...  21.2 us
    all_to_all x1, waiting for transfers between devices, shards(): lax.all_to_all(first_section(sent_input), 'ctx', split_axis=1, concat_axi...  20.2 us
    reduce_scatter x1, waiting for transfers between devices, shards(): lax.psum_scatter(lax.dot_general(w_out, gated, (((0,), (1,)), ((), ())),...  18.8 us
    all_to_all x1, blocking collectives, shards(): lax.all_to_all(returned, 'ctx', split_axis=0, concat_axis=1, tiled=True)  14.8 us
    dot_general x12, matrix products, cycle_apply(): return jnp.einsum('kn,zmnc->zmkc', table, operand, precision=precise)  12.8 us
    all_to_all x1, waiting for transfers between devices, shards(): lax.all_to_all(gated_in.reshape(1, ctx_size, per_dev, chan_width), 'ctx',...  7.8 us
    all_to_all x1, starting transfers between devices, shards(): lax.all_to_all(gated_in.reshape(1, ctx_size, per_dev, chan_width), 'ctx',...  7.36 us
  transfers between devices with their start and end apart: 5, of which 5 were waited for; matrix products, arithmetic and copies ran while one was open for 3% of the time, Pallas kernels for 0%

commit v1 on v0

--- a/solution.py
+++ b/solution.py
@@ -99,7 +99,10 @@
     def last_apply(table, operand):
         return jnp.einsum("nk,kzmc->nzmc", table, operand, precision=precise)
 
-    portion = lax.all_to_all(turned, "ctx", split_axis=2, concat_axis=1, tiled=True)
+    portion = jnp.concatenate(
+        lax.all_to_all(jnp.stack(jnp.split(turned, lax.axis_size("ctx"), axis=2)), "ctx", 0, 0),
+        axis=1,
+    )
     returned = last_apply(last_cos, portion[0]) - last_apply(last_sin, portion[1])
     convolved = lax.all_to_all(returned, "ctx", split_axis=0, concat_axis=1, tiled=True).reshape(
         tok_rows, chan_width

time: 181 us -> 181 us (level)
  no operation moved by 1% of the time
where the time goes in v1:
time: 181 us
  waiting for transfers between devices  74.9 us (41%)
  blocking collectives  46.6 us (26%)
  starting transfers between devices  21.6 us (12%)
  matrix products  17.9 us (10%)
  between operations  13.8 us (8%)
  other arithmetic  4.2 us (2%)
    all_to_all x1, blocking collectives, shards(): lax.all_to_all(jnp.stack(jnp.split(turned, lax.axis_size('ctx'), axis=2))...  31.8 us
    all_to_all x1, waiting for transfers between devices, shards(): lax.all_to_all(first_section(sent_filter), 'ctx', split_axis=1, concat_ax...  21.2 us
    all_to_all x1, waiting for transfers between devices, shards(): lax.all_to_all(first_section(sent_input), 'ctx', split_axis=1, concat_axi...  20.2 us
    reduce_scatter x1, waiting for transfers between devices, shards(): lax.psum_scatter(lax.dot_general(w_out, gated, (((0,), (1,)), ((), ())),...  18.8 us
    all_to_all x1, blocking collectives, shards(): lax.all_to_all(returned, 'ctx', split_axis=0, concat_axis=1, tiled=True)  14.8 us
    dot_general x12, matrix products, cycle_apply(): return jnp.einsum('kn,zmnc->zmkc', table, operand, precision=precise)  12.8 us
    all_to_all x1, waiting for transfers between devices, shards(): lax.all_to_all(gated_in.reshape(1, ctx_size, per_dev, chan_width), 'ctx',...  7.8 us
    all_to_all x1, starting transfers between devices, shards(): lax.all_to_all(gated_in.reshape(1, ctx_size, per_dev, chan_width), 'ctx',...  7.36 us
  transfers between devices with their start and end apart: 5, of which 5 were waited for; matrix products, arithmetic and copies ran while one was open for 3% of the time, Pallas kernels for 0%

profile of v1, /device:TPU:0, one launch (start us, length us, event | category | flops | bytes accessed | tf_op | source)
XLA Modules:
  0.0 180.8 jit_solution(16473921402815745993)
XLA Ops:
  6.5 1.7 fusion.66
  8.2 7.4 %all-to-all-start = ((bf16[1,16,8,512]{3,2,0,1:T(8,128)(2,1)}), bf16[1,16,8,512]{3,2,0,1:T(8,128)(2,1)S(1)}, u32[]{:S(2)}, u32[]{:S(2)}) async-start(bf16[1,16,8,512]{3,2,0,1:T(8,128)(2,1)} %fusion.66), calls=%async_computation | async-start | bytes 262144 | tf_op jit(solution)/shard_map/all_to_all | solution.py:31
  15.7 7.8 %all-to-all-done = bf16[1,16,8,512]{3,2,0,1:T(8,128)(2,1)S(1)} async-done(((bf16[1,16,8,512]{3,2,0,1:T(8,128)(2,1)}), bf16[1,16,8,512]{3,2,0,1:T(8,128)(2,1)S(1)}, u32[]{:S(2)}, u32[]{:S(2)}) %all-to-all-start) | async-done | bytes 131104 | tf_op jit(solution)/shard_map/all_to_all | solution.py:31
  23.5 3.5 %all-to-all-start.2 = ((bf16[1,16,8,512]{3,2,0,1:T(8,128)(2,1)}), bf16[1,16,8,512]{3,2,0,1:T(8,128)(2,1)S(1)}, u32[]{:S(2)}, u32[]{:S(2)}) async-start(bf16[1,16,8,512]{3,2,0,1:T(8,128)(2,1)} %bitcast.228), calls=%async_computation.2 | async-start | bytes 262144 | tf_op jit(solution)/shard_map/all_to_all | solution.py:38
  27.0 0.5 convolution_negate_fusion.1
  27.5 0.5 fusion.24
  28.0 6.9 %all-to-all-done.2 = bf16[1,16,8,512]{3,2,0,1:T(8,128)(2,1)S(1)} async-done(((bf16[1,16,8,512]{3,2,0,1:T(8,128)(2,1)}), bf16[1,16,8,512]{3,2,0,1:T(8,128)(2,1)S(1)}, u32[]{:S(2)}, u32[]{:S(2)}) %all-to-all-start.2) | async-done | bytes 131104 | tf_op jit(solution)/shard_map/all_to_all | solution.py:38
  35.4 0.6 multiply_add_fusion.1
  36.7 1.1 pad_maximum_fusion.1
  37.8 3.7 %all-to-all-start.3 = ((f32[2,16,2,8,512]{4,3,2,0,1:T(8,128)}), f32[2,16,2,8,512]{4,3,2,0,1:T(8,128)S(1)}, u32[]{:S(2)}, u32[]{:S(2)}) async-start(f32[2,16,2,8,512]{4,3,2,0,1:T(8,128)} %pad_maximum_fusion.1), calls=%async_computation.3 | async-start | bytes 2097152 | tf_op jit(solution)/shard_map/all_to_all | solution.py:69
  42.1 1.1 pad_maximum_fusion
  43.1 21.2 %all-to-all-done.3 = f32[2,16,2,8,512]{4,3,2,0,1:T(8,128)S(1)} async-done(((f32[2,16,2,8,512]{4,3,2,0,1:T(8,128)}), f32[2,16,2,8,512]{4,3,2,0,1:T(8,128)S(1)}, u32[]{:S(2)}, u32[]{:S(2)}) %all-to-all-start.3) | async-done | bytes 1048608 | tf_op jit(solution)/shard_map/all_to_all | solution.py:69
  64.3 6.8 %all-to-all-start.1 = ((f32[2,16,2,8,512]{4,3,2,0,1:T(8,128)}), f32[2,16,2,8,512]{4,3,2,0,1:T(8,128)S(1)}, u32[]{:S(2)}, u32[]{:S(2)}) async-start(f32[2,16,2,8,512]{4,3,2,0,1:T(8,128)} %pad_maximum_fusion), calls=%async_computation.1 | async-start | bytes 2097152 | tf_op jit(solution)/shard_map/all_to_all | solution.py:66
  71.6 1.1 fusion.16
  72.7 1.1 fusion.15
  73.8 20.2 %all-to-all-done.1 = f32[2,16,2,8,512]{4,3,2,0,1:T(8,128)S(1)} async-done(((f32[2,16,2,8,512]{4,3,2,0,1:T(8,128)}), f32[2,16,2,8,512]{4,3,2,0,1:T(8,128)S(1)}, u32[]{:S(2)}, u32[]{:S(2)}) %all-to-all-start.1) | async-done | bytes 1048608 | tf_op jit(solution)/shard_map/all_to_all | solution.py:66
  94.2 1.1 fusion.14
  95.3 1.1 fusion.13
  96.4 1.1 convolution_subtract_fusion.1
  97.5 1.1 convolution_add_fusion.1
  98.7 1.1 convolution_add_fusion.2
  99.8 1.1 multiply_subtract_fusion
  100.9 0.9 fusion.8
  101.8 0.9 fusion.10
  102.7 0.9 fusion.1
  103.6 1.2 subtract_bitcast_fusion
  105.1 31.8 %all_to_all.62 = f32[16,2,2,1,8,512]{5,4,2,1,3,0:T(8,128)S(1)} all-to-all(f32[16,2,2,1,8,512]{5,4,2,1,3,0:T(8,128)S(1)} %fusion.50), channel_id=1, replica_groups=mesh['ctx'=16,'chan'=2] {'ctx'}, dimensions={0} | all-to-all | bytes 2097152 | tf_op jit(solution)/shard_map/all_to_all | solution.py:103
  137.0 0.7 fusion.5
  137.7 0.7 fusion.3
  138.5 14.8 %all_to_all.63 = f32[16,1,8,512]{3,2,1,0:T(8,128)S(1)} all-to-all(f32[16,1,8,512]{3,2,1,0:T(8,128)S(1)} %copy.107), channel_id=1, replica_groups=mesh['ctx'=16,'chan'=2] {'ctx'}, dimensions={0} | all-to-all | bytes 524288 | tf_op jit(solution)/shard_map/all_to_all | solution.py:107
  153.4 1.7 fusion
  155.1 18.8 %reduce-scatter.2.cloned.1.call-done = bf16[2048,128]{0,1:T(8,128)(2,1)} async-done(((bf16[4096,128]{0,1:T(8,128)(2,1)}), bf16[2048,128]{0,1:T(8,128)(2,1)}) %reduce-scatter.2.cloned.1.call-update) | async-done | bytes 524304 | tf_op jit(solution)/shard_map/reduce_scatter | solution.py:114
  (41 shorter events, 2.8 us)
Async XLA Ops:
  8.2 15.3 %all-to-all-start = ((bf16[1,16,8,512]{3,2,0,1:T(8,128)(2,1)}), bf16[1,16,8,512]{3,2,0,1:T(8,128)(2,1)S(1)}, u32[]{:S(2)}, u32[]{:S(2)}) async-start(bf16[1,16,8,512]{3,2,0,1:T(8,128)(2,1)} %fusion.66), calls=%async_computation | async-start | bytes 262144 | tf_op jit(solution)/shard_map/all_to_all | solution.py:31
  23.5 11.4 %all-to-all-start.2 = ((bf16[1,16,8,512]{3,2,0,1:T(8,128)(2,1)}), bf16[1,16,8,512]{3,2,0,1:T(8,128)(2,1)S(1)}, u32[]{:S(2)}, u32[]{:S(2)}) async-start(bf16[1,16,8,512]{3,2,0,1:T(8,128)(2,1)} %bitcast.228), calls=%async_computation.2 | async-start | bytes 262144 | tf_op jit(solution)/shard_map/all_to_all | solution.py:38
  37.8 26.6 %all-to-all-start.3 = ((f32[2,16,2,8,512]{4,3,2,0,1:T(8,128)}), f32[2,16,2,8,512]{4,3,2,0,1:T(8,128)S(1)}, u32[]{:S(2)}, u32[]{:S(2)}) async-start(f32[2,16,2,8,512]{4,3,2,0,1:T(8,128)} %pad_maximum_fusion.1), calls=%async_computation.3 | async-start | bytes 2097152 | tf_op jit(solution)/shard_map/all_to_all | solution.py:69
  64.3 29.8 %all-to-all-start.1 = ((f32[2,16,2,8,512]{4,3,2,0,1:T(8,128)}), f32[2,16,2,8,512]{4,3,2,0,1:T(8,128)S(1)}, u32[]{:S(2)}, u32[]{:S(2)}) async-start(f32[2,16,2,8,512]{4,3,2,0,1:T(8,128)} %pad_maximum_fusion), calls=%async_computation.1 | async-start | bytes 2097152 | tf_op jit(solution)/shard_map/all_to_all | solution.py:66
  71.1 102.8 %reduce-scatter.2.cloned.1.call-start = ((), (), s32[]{:S(2)}) async-start(), calls=%async_computation.7 | async-start | bytes 1572864 | tf_op jit(solution)/shard_map/reduce_scatter | solution.py:114
  105.1 48.3 %copy-start = (bf16[512,4096]{1,0:T(8,128)(2,1)S(1)}, bf16[512,4096]{1,0:T(8,128)(2,1)}, u32[]{:S(2)}) copy-start(bf16[512,4096]{1,0:T(8,128)(2,1)} %param.11) | copy-start | bytes 12582916
  105.1 48.3 %copy-start.1 = (bf16[128,512]{1,0:T(8,128)(2,1)S(1)}, bf16[128,512]{1,0:T(8,128)(2,1)}, u32[]{:S(2)}) copy-start(bf16[128,512]{1,0:T(8,128)(2,1)} %param.8) | copy-start | bytes 393220
  105.1 48.3 %copy-start.2 = (bf16[128,512]{1,0:T(8,128)(2,1)S(1)}, bf16[128,512]{1,0:T(8,128)(2,1)}, u32[]{:S(2)}) copy-start(bf16[128,512]{1,0:T(8,128)(2,1)} %param.7) | copy-start | bytes 393220
  105.1 48.3 %copy-start.3 = (bf16[128,512]{1,0:T(8,128)(2,1)S(1)}, bf16[128,512]{1,0:T(8,128)(2,1)}, u32[]{:S(2)}) copy-start(bf16[128,512]{1,0:T(8,128)(2,1)} %param.6) | copy-start | bytes 393220
  105.1 48.3 %copy-start.4 = (f32[512]{0:T(512)S(1)}, f32[512]{0:T(512)}, u32[]{:S(2)}) copy-start(f32[512]{0:T(512)} %param.10) | copy-start | bytes 6148
Sparse Core Ops, SparseCore 0:
  155.3 18.6 reduce-scatter.1
